TPU v7x, 128 devices: a whole 4x4x4 slice. The times are simulated.
128 devices in a mesh: row: 8 (over x, core), col: 16 (over z, y).
Axes of the slice: x: 4, y: 4, z: 4, core: 2. Of those that a mesh axis runs over, the one named last changes fastest.
Arguments:
- surface_head: float32 [512, 4096], P('row', 'col'), may hold values from -6 to 6
- conduct_x: float32 [512, 4096], P('row', 'col'), may hold values from 0.01 to 0.1
- conduct_y: float32 [512, 4096], P('row', 'col'), may hold values from 0.01 to 0.1
- porosity: float32 [512, 4096], P('row', 'col'), may hold values from 0.45 to 1
- rainfall: float32 [512, 4096], P('row', 'col'), may hold values from 0.005 to 0.1
- pipe_head: float32 [32, 32768], P(None, ('row', 'col')), may hold values from -6 to 6
- pipe_class: int32 [32768], P(('row', 'col')), may hold values from 0 to 3
- pipe_up: int32 [32768], P(('row', 'col')), may hold values from 0 to 4095
- pipe_down: int32 [32768], P(('row', 'col')), may hold values from 0 to 4095
- pipe_matrices: float32 [4, 32, 32], replicated
- link_cell: int32 [128, 128, 64], P(('row', 'col')), may hold values from -1 to 16383, as said below
- link_node: int32 [128, 128, 64], P(None, ('row', 'col')), may hold values from -1 to 8191, as said below
- link_coef: float32 [128, 128, 64], P(None, ('row', 'col')), may hold values from 0.05 to 0.4
Outputs:
- surface_out: float32 [512, 4096], P('row', 'col')
- pipe_out: float32 [32, 32768], P(None, ('row', 'col'))
Inputs may be any that keep to these rules, and one draw needn't show every extreme that they name: `link_cell`: for each source tile and pipe owner the live slots come first; each is a cell of the source tile counted row by row; the other slots are -1. In every draw some tile sends 64 live slots to some owner. `link_node`: -1 exactly where link_cell is -1 at the same source tile, owner and slot; else a node of the owner's pipes, numbered node * 256 + pipe.
All inputs are finite; a program needn't handle non-finite values.
Results may differ from a plain program's by a relative error of at most 0.00015.
Values sent between devices are 32-bit elements; how exact they have to be, the bound alone decides.
No kernel may reach another device: no remote copies, remote signals or barrier semaphores. Data moves between devices by JAX's collectives and lax.ppermute only.
A program may use at most 64 MiB of HBM per device.

v0:
```python
import jax
import jax.numpy as jnp
from jax import lax
from jax.sharding import PartitionSpec as P

CLASSES = 4
SWEEPS = 4
STEPS = 3
boundary_gain = 0.5


def passed_along(block, axis, distance):
    devices = range(lax.axis_size(axis))
    route = [(i - distance, i) for i in devices if i - distance in devices]
    return lax.ppermute(block, axis, route)


def with_halo(block, sides, width):
    for axis, dim in sides:
        count = lax.axis_size(axis)
        forward = [(i, i + 1) for i in range(count - 1)]
        backward = [(target, source) for source, target in forward]
        low = lax.ppermute(
            lax.slice_in_dim(block, block.shape[dim] - width, None, axis=dim), axis, forward
        )
        high = lax.ppermute(lax.slice_in_dim(block, 0, width, axis=dim), axis, backward)
        block = jnp.concatenate([low, block, high], axis=dim)
    return block


def sweep_once(
    center, north, south, west, east, north_gain, south_gain, west_gain, east_gain, inverse, source
):
    change = (
        north_gain * (north - center)
        + south_gain * (south - center)
        + west_gain * (west - center)
        + east_gain * (east - center)
    )
    return center + change * inverse + source


def body(
    surface_head,
    conduct_x,
    conduct_y,
    porosity,
    rainfall,
    pipe_head,
    pipe_class,
    pipe_up,
    pipe_down,
    pipe_matrices,
    link_cell,
    link_node,
    link_coef,
):
    tile_rows, tile_cols = surface_head.shape
    inverse = 1.0 / porosity
    from_above = passed_along(conduct_x[-1:, :], "row", 1)
    north_gain = jnp.concatenate([from_above, conduct_x[:-1, :]], axis=0)
    from_left = passed_along(conduct_y[:, -1:], "col", 1)
    west_gain = jnp.concatenate([from_left, conduct_y[:, :-1]], axis=1)
    cell_index = link_cell[0]
    cell_live = cell_index >= 0
    cell_safe = jnp.where(cell_live, cell_index, 0)
    node_index = link_node[:, 0, :]
    node_live = node_index >= 0
    node_safe = jnp.where(node_live, node_index, 0)
    link_gain = link_coef[:, 0, :]
    inverse_flat = inverse.reshape(-1)
    surface = surface_head
    pipe_state = pipe_head
    for coupling_step in range(STEPS):
        for sweep_index in range(SWEEPS):
            padded = with_halo(surface, (("row", 0), ("col", 1)), 1)
            surface = sweep_once(
                surface,
                padded[:-2, 1:-1],
                padded[2:, 1:-1],
                padded[1:-1, :-2],
                padded[1:-1, 2:],
                north_gain,
                conduct_x,
                west_gain,
                conduct_y,
                inverse,
                rainfall,
            )
        surface_flat = surface.reshape(-1)
        sent_heads = jnp.where(cell_live, surface_flat[cell_safe], 0.0)
        pipe_flat = pipe_state.reshape(-1)
        pipe_at_slots = jnp.where(node_live, pipe_flat[node_safe], 0.0)
        arrived = lax.all_to_all(
            sent_heads, ("row", "col"), split_axis=0, concat_axis=0, tiled=True
        )
        manhole_flow = jnp.where(node_live, link_gain * (arrived - pipe_at_slots), 0.0)
        inflow = jnp.zeros_like(pipe_flat).at[node_safe].add(manhole_flow).reshape(pipe_state.shape)
        returned = lax.all_to_all(
            manhole_flow, ("row", "col"), split_axis=0, concat_axis=0, tiled=True
        )
        surface = (
            surface_flat.at[cell_safe]
            .add(-(returned * inverse_flat[cell_safe]))
            .reshape(tile_rows, tile_cols)
        )
        first_heads, last_heads = (
            lax.all_gather(pipe_state[0], "col", axis=0, tiled=True),
            lax.all_gather(pipe_state[-1], "col", axis=0, tiled=True),
        )
        balance = pipe_state + inflow
        balance = balance.at[0].add(boundary_gain * last_heads[pipe_up])
        balance = balance.at[-1].add(boundary_gain * first_heads[pipe_down])
        updated = jnp.zeros_like(pipe_state)
        for class_index in range(CLASSES):
            product = jnp.dot(
                pipe_matrices[class_index],
                balance,
                precision=lax.Precision.HIGHEST,
                preferred_element_type=jnp.float32,
            )
            updated = jnp.where(pipe_class[None, :] == class_index, product, updated)
        pipe_state = updated
    return (surface, pipe_state)


def solution(mesh):
    placed = (
        P("row", "col"),
        P("row", "col"),
        P("row", "col"),
        P("row", "col"),
        P("row", "col"),
        P(None, ("row", "col")),
        P(("row", "col")),
        P(("row", "col")),
        P(("row", "col")),
        P(),
        P(("row", "col"), None, None),
        P(None, ("row", "col"), None),
        P(None, ("row", "col"), None),
    )
    return jax.shard_map(
        body,
        mesh=mesh,
        in_specs=placed,
        out_specs=(P("row", "col"), P(None, ("row", "col"))),
        check_vma=False,
    )
```

profile of v0, /device:TPU:1, one launch (start us, length us, event | category | flops | bytes accessed | tf_op | source)
XLA Modules:
  0.0 1038.9 jit_solution(1538303368657251957)
XLA Ops:
  38.3 23.2 %all-gather = f32[1,4096]{1,0:T(1,128)S(1)} all-gather(f32[1,256]{1,0:T(1,128)S(1)} %get-tuple-element.133), channel_id=2, replica_groups=mesh['row'=8,'col'=16] {'col'}, dimensions={1}, use_global_device_ids=true | all-gather | bytes 17408 | tf_op jit(solution)/shard_map/all_gather | solution.py:109
  96.8 19.4 %all-gather.1 = f32[1,4096]{1,0:T(1,128)S(1)} all-gather(f32[1,256]{1,0:T(1,128)S(1)} %get-tuple-element.132), channel_id=3, replica_groups=mesh['row'=8,'col'=16] {'col'}, dimensions={1}, use_global_device_ids=true | all-gather | bytes 17408 | tf_op jit(solution)/shard_map/all_gather | solution.py:108
  118.2 45.5 %gather_fusion = f32[8192]{0:T(1024)S(1)} fusion(f32[16384]{0:T(1024)S(1)} %bitcast.123, s32[8192]{0:T(1024)S(1)} %broadcast_clamp_fusion.1), kind=kCustom, calls=%fused_computation | custom fusion | bytes 98304 | tf_op jit(solution)/shard_map/gather | solution.py:91
  164.5 12.9 %all-to-all-start = ((f32[128,1,64]{2,1,0:T(1,128)}), f32[128,1,64]{2,1,0:T(1,128)S(1)}, u32[]{:S(2)}, u32[]{:S(2)}) async-start(f32[128,1,64]{2,1,0:T(1,128)} %bitcast.2), calls=%async_computation | async-start | bytes 131072 | tf_op jit(solution)/shard_map/all_to_all | solution.py:94
  177.5 45.5 %gather_fusion.1 = f32[8192]{0:T(1024)S(1)} fusion(f32[8192]{0:T(1024)S(1)} %bitcast.130, s32[8192]{0:T(1024)S(1)} %broadcast_clamp_fusion), kind=kCustom, calls=%fused_computation.1 | custom fusion | bytes 98304 | tf_op jit(solution)/shard_map/gather | solution.py:93
  224.1 45.5 %gather_fusion.2 = f32[8192]{0:T(1024)S(1)} fusion(f32[16384]{0:T(1024)S(1)} %bitcast.132, s32[8192]{0:T(1024)S(1)} %broadcast_clamp_fusion.1), kind=kCustom, calls=%fused_computation.2 | custom fusion | bytes 98304 | tf_op jit(solution)/shard_map/gather | solution.py:104
  280.2 44.9 %scatter_custom_fusion.1 = f32[8192]{0:T(1024)S(1)} fusion(s32[8192]{0:T(1024)S(1)} %reshape.369, f32[8192]{0:T(1024)S(1)} %reshape.475, f32[]{:T(128)} %constant.152.clone.1), kind=kCustom, calls=%fused_computation.362 | custom fusion | flops 8192 | bytes 32772 | tf_op jit(solution)/shard_map/scatter-add | solution.py:98
  325.3 50.3 %scatter_fusion = f32[16384]{0:T(1024)S(1)} fusion(f32[16384]{0:T(1024)S(1)} %bitcast.124, s32[8192]{0:T(1024)S(1)} %reshape.465, f32[8192]{0:T(1024)S(1)} %reshape.467), kind=kCustom, calls=%fused_computation.13 | custom fusion | flops 8192 | bytes 131072 | tf_op jit(solution)/shard_map/scatter-add | solution.py:104
  383.4 9.8 collective-permute-start.20
  422.8 25.7 %all-gather.2 = f32[1,4096]{1,0:T(1,128)S(1)} all-gather(f32[1,256]{1,0:T(1,128)S(1)} %get-tuple-element.131), channel_id=4, replica_groups=mesh['row'=8,'col'=16] {'col'}, dimensions={1}, use_global_device_ids=true | all-gather | bytes 17408 | tf_op jit(solution)/shard_map/all_gather | solution.py:109
  468.7 17.2 %all-gather.3 = f32[1,4096]{1,0:T(1,128)S(1)} all-gather(f32[1,256]{1,0:T(1,128)S(1)} %get-tuple-element.130), channel_id=5, replica_groups=mesh['row'=8,'col'=16] {'col'}, dimensions={1}, use_global_device_ids=true | all-gather | bytes 17408 | tf_op jit(solution)/shard_map/all_gather | solution.py:108
  487.8 45.5 %gather_fusion.3 = f32[8192]{0:T(1024)S(1)} fusion(f32[16384]{0:T(1024)S(1)} %bitcast.125, s32[8192]{0:T(1024)S(1)} %broadcast_clamp_fusion.1), kind=kCustom, calls=%fused_computation.3 | custom fusion | bytes 98304 | tf_op jit(solution)/shard_map/gather | solution.py:91
  534.1 13.1 %all-to-all-start.2 = ((f32[128,1,64]{2,1,0:T(1,128)}), f32[128,1,64]{2,1,0:T(1,128)S(1)}, u32[]{:S(2)}, u32[]{:S(2)}) async-start(f32[128,1,64]{2,1,0:T(1,128)} %bitcast.9), calls=%async_computation.2 | async-start | bytes 131072 | tf_op jit(solution)/shard_map/all_to_all | solution.py:94
  547.2 45.5 %gather_fusion.6 = f32[8192]{0:T(1024)S(1)} fusion(f32[8192]{0:T(1024)S(1)} %bitcast.131, s32[8192]{0:T(1024)S(1)} %broadcast_clamp_fusion), kind=kCustom, calls=%fused_computation.6 | custom fusion | bytes 98304 | tf_op jit(solution)/shard_map/gather | solution.py:93
  603.4 44.9 %scatter_custom_fusion.3 = f32[8192]{0:T(1024)S(1)} fusion(s32[8192]{0:T(1024)S(1)} %reshape.369, f32[8192]{0:T(1024)S(1)} %reshape.491, f32[]{:T(128)} %constant.152.clone.1), kind=kCustom, calls=%fused_computation.360 | custom fusion | flops 8192 | bytes 32772 | tf_op jit(solution)/shard_map/scatter-add | solution.py:98
  648.6 50.3 %scatter_fusion.1 = f32[16384]{0:T(1024)S(1)} fusion(f32[16384]{0:T(1024)S(1)} %bitcast.126, s32[8192]{0:T(1024)S(1)} %reshape.465, f32[8192]{0:T(1024)S(1)} %reshape.483), kind=kCustom, calls=%fused_computation.15 | custom fusion | flops 8192 | bytes 131072 | tf_op jit(solution)/shard_map/scatter-add | solution.py:104
  746.0 25.7 %all-gather.4 = f32[1,4096]{1,0:T(1,128)S(1)} all-gather(f32[1,256]{1,0:T(1,128)S(1)} %get-tuple-element.129), channel_id=6, replica_groups=mesh['row'=8,'col'=16] {'col'}, dimensions={1}, use_global_device_ids=true | all-gather | bytes 17408 | tf_op jit(solution)/shard_map/all_gather | solution.py:109
  791.9 17.2 %all-gather.5 = f32[1,4096]{1,0:T(1,128)S(1)} all-gather(f32[1,256]{1,0:T(1,128)S(1)} %get-tuple-element.128), channel_id=7, replica_groups=mesh['row'=8,'col'=16] {'col'}, dimensions={1}, use_global_device_ids=true | all-gather | bytes 17408 | tf_op jit(solution)/shard_map/all_gather | solution.py:108
  811.0 45.5 %gather_fusion.7 = f32[8192]{0:T(1024)S(1)} fusion(f32[16384]{0:T(1024)S(1)} %bitcast.127, s32[8192]{0:T(1024)S(1)} %broadcast_clamp_fusion.1), kind=kCustom, calls=%fused_computation.7 | custom fusion | bytes 98304 | tf_op jit(solution)/shard_map/gather | solution.py:91
  857.3 13.1 %all-to-all-start.4 = ((f32[128,1,64]{2,1,0:T(1,128)}), f32[128,1,64]{2,1,0:T(1,128)S(1)}, u32[]{:S(2)}, u32[]{:S(2)}) async-start(f32[128,1,64]{2,1,0:T(1,128)} %bitcast.27), calls=%async_computation.4 | async-start | bytes 131072 | tf_op jit(solution)/shard_map/all_to_all | solution.py:94
  870.4 45.5 %gather_fusion.10 = f32[8192]{0:T(1024)S(1)} fusion(f32[8192]{0:T(1024)S(1)} %bitcast.129, s32[8192]{0:T(1024)S(1)} %broadcast_clamp_fusion), kind=kCustom, calls=%fused_computation.10 | custom fusion | bytes 98304 | tf_op jit(solution)/shard_map/gather | solution.py:93
  916.2 44.9 %scatter_custom_fusion.5 = f32[8192]{0:T(1024)S(1)} fusion(s32[8192]{0:T(1024)S(1)} %reshape.369, f32[8192]{0:T(1024)S(1)} %reshape.507, f32[]{:T(128)} %constant.152.clone.1), kind=kCustom, calls=%fused_computation.358 | custom fusion | flops 8192 | bytes 32772 | tf_op jit(solution)/shard_map/scatter-add | solution.py:98
  962.4 15.8 %all-to-all-start.5 = ((f32[128,1,64]{2,1,0:T(1,128)}), f32[128,1,64]{2,1,0:T(1,128)S(1)}, u32[]{:S(2)}, u32[]{:S(2)}) async-start(f32[128,1,64]{2,1,0:T(1,128)} %bitcast.35), calls=%async_computation.5 | async-start | bytes 131072 | tf_op jit(solution)/shard_map/all_to_all | solution.py:99
  988.0 50.3 %scatter_fusion.2 = f32[16384]{0:T(1024)S(1)} fusion(f32[16384]{0:T(1024)S(1)} %bitcast.128, s32[8192]{0:T(1024)S(1)} %reshape.465, f32[8192]{0:T(1024)S(1)} %reshape.499), kind=kCustom, calls=%fused_computation.17 | custom fusion | flops 8192 | bytes 131072 | tf_op jit(solution)/shard_map/scatter-add | solution.py:104
  (283 shorter events, 239.3 us)
Async XLA Ops:
  1.4 17.1 %collective-permute-start.2 = (f32[1,256]{1,0:T(1,128)S(1)}, f32[1,256]{1,0:T(1,128)S(1)}, u32[]{:S(2)}, u32[]{:S(2)}) collective-permute-start(f32[1,256]{1,0:T(1,128)S(1)} %get-tuple-element.127), channel_id=1, source_target_pairs={{16,0},{32,16},{48,32},{64,48},{80,64},{96,80},{112,96},{17,1},{33... | collective-permute-start | bytes 3080 | tf_op jit(solution)/shard_map/ppermute | solution.py:26
  4.7 13.8 %collective-permute-start.1 = (f32[1,256]{1,0:T(1,128)S(1)}, f32[1,256]{1,0:T(1,128)S(1)}, u32[]{:S(2)}, u32[]{:S(2)}) collective-permute-start(f32[1,256]{1,0:T(1,128)S(1)} %get-tuple-element.126), channel_id=1, source_target_pairs={{0,16},{16,32},{32,48},{48,64},{64,80},{80,96},{96,112},{1,17},{17... | collective-permute-start | bytes 3080 | tf_op jit(solution)/shard_map/ppermute | solution.py:23
  8.5 15.5 %collective-permute-start = (f32[1,256]{1,0:T(1,128)S(1)}, f32[1,256]{1,0:T(1,128)S(1)}, u32[]{:S(2)}, u32[]{:S(2)}) collective-permute-start(f32[1,256]{1,0:T(1,128)S(1)} %slice.500), channel_id=1, source_target_pairs={{0,16},{16,32},{32,48},{48,64},{64,80},{80,96},{96,112},{1,17},{17... | collective-permute-start | bytes 3080 | tf_op jit(solution)/shard_map/ppermute | solution.py:15
  32.4 30.8 %collective-permute-start.9 = (f32[66,1]{1,0:T(8,128)S(1)}, f32[66,1]{1,0:T(8,128)S(1)}, u32[]{:S(2)}, u32[]{:S(2)}) collective-permute-start(f32[66,1]{1,0:T(8,128)S(1)} %get-tuple-element.101), channel_id=1, source_target_pairs={{1,0},{2,1},{3,2},{4,3},{5,4},{6,5},{7,6},{8,7},{9,8},{10,9},{11,1... | collective-permute-start | bytes 800 | tf_op jit(solution)/shard_map/ppermute | solution.py:26
  33.7 29.5 %collective-permute-start.8 = (f32[66,1]{1,0:T(8,128)S(1)}, f32[66,1]{1,0:T(8,128)S(1)}, u32[]{:S(2)}, u32[]{:S(2)}) collective-permute-start(f32[66,1]{1,0:T(8,128)S(1)} %get-tuple-element.100), channel_id=1, source_target_pairs={{0,1},{1,2},{2,3},{3,4},{4,5},{5,6},{6,7},{7,8},{8,9},{9,10},{10,1... | collective-permute-start | bytes 800 | tf_op jit(solution)/shard_map/ppermute | solution.py:23
  63.3 12.2 %collective-permute-start.11 = (f32[1,256]{1,0:T(1,128)S(1)}, f32[1,256]{1,0:T(1,128)S(1)}, u32[]{:S(2)}, u32[]{:S(2)}) collective-permute-start(f32[1,256]{1,0:T(1,128)S(1)} %get-tuple-element.123), channel_id=1, source_target_pairs={{16,0},{32,16},{48,32},{64,48},{80,64},{96,80},{112,96},{17,1},{33... | collective-permute-start | bytes 3080 | tf_op jit(solution)/shard_map/ppermute | solution.py:26
  90.9 27.1 %collective-permute-start.17 = (f32[66,1]{1,0:T(8,128)S(1)}, f32[66,1]{1,0:T(8,128)S(1)}, u32[]{:S(2)}, u32[]{:S(2)}) collective-permute-start(f32[66,1]{1,0:T(8,128)S(1)} %get-tuple-element.97), channel_id=1, source_target_pairs={{1,0},{2,1},{3,2},{4,3},{5,4},{6,5},{7,6},{8,7},{9,8},{10,9},{11,1... | collective-permute-start | bytes 800 | tf_op jit(solution)/shard_map/ppermute | solution.py:26
  92.2 25.8 %collective-permute-start.16 = (f32[66,1]{1,0:T(8,128)S(1)}, f32[66,1]{1,0:T(8,128)S(1)}, u32[]{:S(2)}, u32[]{:S(2)}) collective-permute-start(f32[66,1]{1,0:T(8,128)S(1)} %get-tuple-element.96), channel_id=1, source_target_pairs={{0,1},{1,2},{2,3},{3,4},{4,5},{5,6},{6,7},{7,8},{8,9},{9,10},{10,1... | collective-permute-start | bytes 800 | tf_op jit(solution)/shard_map/ppermute | solution.py:23
  164.5 105.2 %all-to-all-start = ((f32[128,1,64]{2,1,0:T(1,128)}), f32[128,1,64]{2,1,0:T(1,128)S(1)}, u32[]{:S(2)}, u32[]{:S(2)}) async-start(f32[128,1,64]{2,1,0:T(1,128)} %bitcast.2), calls=%async_computation | async-start | bytes 131072 | tf_op jit(solution)/shard_map/all_to_all | solution.py:94
  270.3 54.9 %all-to-all-start.1 = ((f32[128,1,64]{2,1,0:T(1,128)}), f32[128,1,64]{2,1,0:T(1,128)S(1)}, u32[]{:S(2)}, u32[]{:S(2)}) async-start(f32[128,1,64]{2,1,0:T(1,128)} %bitcast.5), calls=%async_computation.1 | async-start | bytes 131072 | tf_op jit(solution)/shard_map/all_to_all | solution.py:99
  416.9 33.3 %collective-permute-start.29 = (f32[66,1]{1,0:T(8,128)S(1)}, f32[66,1]{1,0:T(8,128)S(1)}, u32[]{:S(2)}, u32[]{:S(2)}) collective-permute-start(f32[66,1]{1,0:T(8,128)S(1)} %get-tuple-element.91), channel_id=1, source_target_pairs={{1,0},{2,1},{3,2},{4,3},{5,4},{6,5},{7,6},{8,7},{9,8},{10,9},{11,1... | collective-permute-start | bytes 800 | tf_op jit(solution)/shard_map/ppermute | solution.py:26
  418.2 32.0 %collective-permute-start.28 = (f32[66,1]{1,0:T(8,128)S(1)}, f32[66,1]{1,0:T(8,128)S(1)}, u32[]{:S(2)}, u32[]{:S(2)}) collective-permute-start(f32[66,1]{1,0:T(8,128)S(1)} %get-tuple-element.90), channel_id=1, source_target_pairs={{0,1},{1,2},{2,3},{3,4},{4,5},{5,6},{6,7},{7,8},{8,9},{9,10},{10,1... | collective-permute-start | bytes 800 | tf_op jit(solution)/shard_map/ppermute | solution.py:23
  450.4 12.2 %collective-permute-start.31 = (f32[1,256]{1,0:T(1,128)S(1)}, f32[1,256]{1,0:T(1,128)S(1)}, u32[]{:S(2)}, u32[]{:S(2)}) collective-permute-start(f32[1,256]{1,0:T(1,128)S(1)} %get-tuple-element.113), channel_id=1, source_target_pairs={{16,0},{32,16},{48,32},{64,48},{80,64},{96,80},{112,96},{17,1},{33... | collective-permute-start | bytes 3080 | tf_op jit(solution)/shard_map/ppermute | solution.py:26
  463.4 24.2 %collective-permute-start.33 = (f32[66,1]{1,0:T(8,128)S(1)}, f32[66,1]{1,0:T(8,128)S(1)}, u32[]{:S(2)}, u32[]{:S(2)}) collective-permute-start(f32[66,1]{1,0:T(8,128)S(1)} %get-tuple-element.89), channel_id=1, source_target_pairs={{1,0},{2,1},{3,2},{4,3},{5,4},{6,5},{7,6},{8,7},{9,8},{10,9},{11,1... | collective-permute-start | bytes 800 | tf_op jit(solution)/shard_map/ppermute | solution.py:26
  464.7 22.9 %collective-permute-start.32 = (f32[66,1]{1,0:T(8,128)S(1)}, f32[66,1]{1,0:T(8,128)S(1)}, u32[]{:S(2)}, u32[]{:S(2)}) collective-permute-start(f32[66,1]{1,0:T(8,128)S(1)} %get-tuple-element.88), channel_id=1, source_target_pairs={{0,1},{1,2},{2,3},{3,4},{4,5},{5,6},{6,7},{7,8},{8,9},{9,10},{10,1... | collective-permute-start | bytes 800 | tf_op jit(solution)/shard_map/ppermute | solution.py:23
  534.1 58.8 %all-to-all-start.2 = ((f32[128,1,64]{2,1,0:T(1,128)}), f32[128,1,64]{2,1,0:T(1,128)S(1)}, u32[]{:S(2)}, u32[]{:S(2)}) async-start(f32[128,1,64]{2,1,0:T(1,128)} %bitcast.9), calls=%async_computation.2 | async-start | bytes 131072 | tf_op jit(solution)/shard_map/all_to_all | solution.py:94
  593.5 54.9 %all-to-all-start.3 = ((f32[128,1,64]{2,1,0:T(1,128)}), f32[128,1,64]{2,1,0:T(1,128)S(1)}, u32[]{:S(2)}, u32[]{:S(2)}) async-start(f32[128,1,64]{2,1,0:T(1,128)} %bitcast.23), calls=%async_computation.3 | async-start | bytes 131072 | tf_op jit(solution)/shard_map/all_to_all | solution.py:99
  740.2 33.3 %collective-permute-start.45 = (f32[66,1]{1,0:T(8,128)S(1)}, f32[66,1]{1,0:T(8,128)S(1)}, u32[]{:S(2)}, u32[]{:S(2)}) collective-permute-start(f32[66,1]{1,0:T(8,128)S(1)} %get-tuple-element.83), channel_id=1, source_target_pairs={{1,0},{2,1},{3,2},{4,3},{5,4},{6,5},{7,6},{8,7},{9,8},{10,9},{11,1... | collective-permute-start | bytes 800 | tf_op jit(solution)/shard_map/ppermute | solution.py:26
  741.5 32.0 %collective-permute-start.44 = (f32[66,1]{1,0:T(8,128)S(1)}, f32[66,1]{1,0:T(8,128)S(1)}, u32[]{:S(2)}, u32[]{:S(2)}) collective-permute-start(f32[66,1]{1,0:T(8,128)S(1)} %get-tuple-element.82), channel_id=1, source_target_pairs={{0,1},{1,2},{2,3},{3,4},{4,5},{5,6},{6,7},{7,8},{8,9},{9,10},{10,1... | collective-permute-start | bytes 800 | tf_op jit(solution)/shard_map/ppermute | solution.py:23
  773.6 12.2 %collective-permute-start.47 = (f32[1,256]{1,0:T(1,128)S(1)}, f32[1,256]{1,0:T(1,128)S(1)}, u32[]{:S(2)}, u32[]{:S(2)}) collective-permute-start(f32[1,256]{1,0:T(1,128)S(1)} %get-tuple-element.105), channel_id=1, source_target_pairs={{16,0},{32,16},{48,32},{64,48},{80,64},{96,80},{112,96},{17,1},{33... | collective-permute-start | bytes 3080 | tf_op jit(solution)/shard_map/ppermute | solution.py:26
  786.6 24.2 %collective-permute-start.49 = (f32[66,1]{1,0:T(8,128)S(1)}, f32[66,1]{1,0:T(8,128)S(1)}, u32[]{:S(2)}, u32[]{:S(2)}) collective-permute-start(f32[66,1]{1,0:T(8,128)S(1)} %get-tuple-element.81), channel_id=1, source_target_pairs={{1,0},{2,1},{3,2},{4,3},{5,4},{6,5},{7,6},{8,7},{9,8},{10,9},{11,1... | collective-permute-start | bytes 800 | tf_op jit(solution)/shard_map/ppermute | solution.py:26
  787.9 22.9 %collective-permute-start.48 = (f32[66,1]{1,0:T(8,128)S(1)}, f32[66,1]{1,0:T(8,128)S(1)}, u32[]{:S(2)}, u32[]{:S(2)}) collective-permute-start(f32[66,1]{1,0:T(8,128)S(1)} %get-tuple-element.80), channel_id=1, source_target_pairs={{0,1},{1,2},{2,3},{3,4},{4,5},{5,6},{6,7},{7,8},{8,9},{9,10},{10,1... | collective-permute-start | bytes 800 | tf_op jit(solution)/shard_map/ppermute | solution.py:23
  857.3 58.8 %all-to-all-start.4 = ((f32[128,1,64]{2,1,0:T(1,128)}), f32[128,1,64]{2,1,0:T(1,128)S(1)}, u32[]{:S(2)}, u32[]{:S(2)}) async-start(f32[128,1,64]{2,1,0:T(1,128)} %bitcast.27), calls=%async_computation.4 | async-start | bytes 131072 | tf_op jit(solution)/shard_map/all_to_all | solution.py:94
  962.4 25.5 %all-to-all-start.5 = ((f32[128,1,64]{2,1,0:T(1,128)}), f32[128,1,64]{2,1,0:T(1,128)S(1)}, u32[]{:S(2)}, u32[]{:S(2)}) async-start(f32[128,1,64]{2,1,0:T(1,128)} %bitcast.35), calls=%async_computation.5 | async-start | bytes 131072 | tf_op jit(solution)/shard_map/all_to_all | solution.py:99
  (45 other events, 312.4 us)
where the time goes:
time: 1040 us
  local copies, waits for them, and re-layouts  339 us (33%)
  other arithmetic  291 us (28%)
  starting transfers between devices  254 us (24%)
  blocking collectives  128 us (12%)
  waiting for transfers between devices  21.3 us (2%)
    scatter-add x3, other arithmetic, body(): surface = surface_flat.at[cell_safe].add(-(returned * inverse_flat[cell_s...  151 us
    gather x9, local copies, waits for them, and re-layouts, body(): pipe_at_slots = jnp.where(node_live, pipe_flat[node_safe], 0.0)  137 us
    gather x6, local copies, waits for them, and re-layouts, body(): sent_heads = jnp.where(cell_live, surface_flat[cell_safe], 0.0)  137 us
    scatter-add x3, other arithmetic, body(): jnp.zeros_like(pipe_flat).at[node_safe].add(manhole_flow)  135 us
    ppermute x24, starting transfers between devices, with_halo(): lax.ppermute(lax.slice_in_dim(block, block.shape[dim] - width, None, axis...  118 us
    all_gather x3, blocking collectives, body(): lax.all_gather(pipe_state[-1], 'col', axis=0, tiled=True)  74.5 us
    ppermute x24, starting transfers between devices, with_halo(): lax.ppermute(lax.slice_in_dim(block, 0, width, axis=dim), axis, backward)  56 us
    all_gather x3, blocking collectives, body(): lax.all_gather(pipe_state[0], 'col', axis=0, tiled=True)  53.8 us
  transfers between devices with their start and end apart: 56, of which 18 were waited for; matrix products, arithmetic and copies ran while one was open for 28% of the time, Pallas kernels for 0%

commit v1 on v0

--- a/solution.py
+++ b/solution.py
@@ -7,6 +7,11 @@
 SWEEPS = 4
 STEPS = 3
 boundary_gain = 0.5
+
+
+def gather_by_exchange(x, axis, dim):
+    copies = jnp.concatenate([x] * lax.axis_size(axis), axis=dim)
+    return lax.all_to_all(copies, axis, dim, dim, tiled=True)
 
 
 def passed_along(block, axis, distance):
@@ -105,7 +110,7 @@
             .reshape(tile_rows, tile_cols)
         )
         first_heads, last_heads = (
-            lax.all_gather(pipe_state[0], "col", axis=0, tiled=True),
+            gather_by_exchange(pipe_state[0], "col", 0),
             lax.all_gather(pipe_state[-1], "col", axis=0, tiled=True),
         )
         balance = pipe_state + inflow

time: 1040 us -> 1010 us (0.971)
  blocking collectives: 128 us -> 74.2 us
  waiting for transfers between devices: 21.3 us -> 48.3 us
    all_gather x3 -> x0, blocking collectives: 53.8 us -> none  [body(): lax.all_gather(pipe_state[0], 'col', axis=0, tiled=True)]
    all_to_all x3, waiting for transfers between devices: 0.01 us -> 27.4 us  [body(): lax.all_to_all(sent_heads, ('row', 'col'), split_axis=0, concat_axis=0, t...]
    all_to_all x3, starting transfers between devices: 35.3 us -> 18.4 us  [body(): lax.all_to_all(manhole_flow, ('row', 'col'), split_axis=0, concat_axis=0,...]
    all_to_all x0 -> x3, starting transfers between devices: none -> 15 us  [gather_by_exchange(): return lax.all_to_all(copies, axis, dim, dim, tiled=True)]
  transfers between devices with their start and end apart: 56 -> 59, of which waited for: 18 -> 20; matrix products, arithmetic and copies ran while one was open for 28% -> 34% of each run, Pallas kernels for 0% -> 0%
where the time goes in v1:
time: 1010 us; the launch traced here: 1000 us
  local copies, waits for them, and re-layouts  340 us (34%)
  other arithmetic  291 us (29%)
  starting transfers between devices  244 us (24%)
  blocking collectives  74.2 us (7%)
  waiting for transfers between devices  48.3 us (5%)
    scatter-add x3, other arithmetic, body(): surface = surface_flat.at[cell_safe].add(-(returned * inverse_flat[cell_s...  151 us
    gather x9, local copies, waits for them, and re-layouts, body(): pipe_at_slots = jnp.where(node_live, pipe_flat[node_safe], 0.0)  137 us
    gather x6, local copies, waits for them, and re-layouts, body(): sent_heads = jnp.where(cell_live, surface_flat[cell_safe], 0.0)  137 us
    scatter-add x3, other arithmetic, body(): jnp.zeros_like(pipe_flat).at[node_safe].add(manhole_flow)  135 us
    ppermute x24, starting transfers between devices, with_halo(): lax.ppermute(lax.slice_in_dim(block, block.shape[dim] - width, None, axis...  118 us
    all_gather x3, blocking collectives, body(): lax.all_gather(pipe_state[-1], 'col', axis=0, tiled=True)  74.2 us
    ppermute x24, starting transfers between devices, with_halo(): lax.ppermute(lax.slice_in_dim(block, 0, width, axis=dim), axis, backward)  56.2 us
    gather x2, local copies, waits for them, and re-layouts, body(): inverse_flat[cell_safe]  45.6 us
  transfers between devices with their start and end apart: 59, of which 20 were waited for; matrix products, arithmetic and copies ran while one was open for 34% of the time, Pallas kernels for 0%

profile of v1, /device:TPU:1, one launch (start us, length us, event | category | flops | bytes accessed | tf_op | source)
XLA Modules:
  0.0 1003.0 jit_solution(121059017126330213)
XLA Ops:
  46.2 22.8 %all-gather = f32[1,4096]{1,0:T(1,128)S(1)} all-gather(f32[1,256]{1,0:T(1,128)S(1)} %get-tuple-element.133), channel_id=2, replica_groups=mesh['row'=8,'col'=16] {'col'}, dimensions={1}, use_global_device_ids=true | all-gather | bytes 17408 | tf_op jit(solution)/shard_map/all_gather | solution.py:114
  97.8 45.5 %gather_fusion.1 = f32[8192]{0:T(1024)S(1)} fusion(f32[8192]{0:T(1024)S(1)} %bitcast.133, s32[8192]{0:T(1024)S(1)} %broadcast_clamp_fusion), kind=kCustom, calls=%fused_computation.1 | custom fusion | bytes 98304 | tf_op jit(solution)/shard_map/gather | solution.py:98
  150.3 45.5 %gather_fusion.2 = f32[8192]{0:T(1024)S(1)} fusion(f32[16384]{0:T(1024)S(1)} %bitcast.135, s32[8192]{0:T(1024)S(1)} %broadcast_clamp_fusion.1), kind=kCustom, calls=%fused_computation.2 | custom fusion | bytes 98304 | tf_op jit(solution)/shard_map/gather | solution.py:109
  196.1 45.5 %gather_fusion = f32[8192]{0:T(1024)S(1)} fusion(f32[16384]{0:T(1024)S(1)} %bitcast.126, s32[8192]{0:T(1024)S(1)} %broadcast_clamp_fusion.1), kind=kCustom, calls=%fused_computation | custom fusion | bytes 98304 | tf_op jit(solution)/shard_map/gather | solution.py:96
  265.8 44.9 %scatter_custom_fusion.1 = f32[8192]{0:T(1024)S(1)} fusion(s32[8192]{0:T(1024)S(1)} %reshape.483, f32[8192]{0:T(1024)S(1)} %reshape.589, f32[]{:T(128)} %constant.152.clone.1), kind=kCustom, calls=%fused_computation.362 | custom fusion | flops 8192 | bytes 32772 | tf_op jit(solution)/shard_map/scatter-add | solution.py:103
  311.0 50.3 %scatter_fusion = f32[16384]{0:T(1024)S(1)} fusion(f32[16384]{0:T(1024)S(1)} %bitcast.127, s32[8192]{0:T(1024)S(1)} %reshape.579, f32[8192]{0:T(1024)S(1)} %reshape.581), kind=kCustom, calls=%fused_computation.13 | custom fusion | flops 8192 | bytes 131072 | tf_op jit(solution)/shard_map/scatter-add | solution.py:109
  369.0 9.8 collective-permute-start.20
  408.4 25.7 %all-gather.1 = f32[1,4096]{1,0:T(1,128)S(1)} all-gather(f32[1,256]{1,0:T(1,128)S(1)} %get-tuple-element.131), channel_id=3, replica_groups=mesh['row'=8,'col'=16] {'col'}, dimensions={1}, use_global_device_ids=true | all-gather | bytes 17408 | tf_op jit(solution)/shard_map/all_gather | solution.py:114
  448.2 45.5 %gather_fusion.6 = f32[8192]{0:T(1024)S(1)} fusion(f32[8192]{0:T(1024)S(1)} %bitcast.134, s32[8192]{0:T(1024)S(1)} %broadcast_clamp_fusion), kind=kCustom, calls=%fused_computation.6 | custom fusion | bytes 98304 | tf_op jit(solution)/shard_map/gather | solution.py:98
  506.6 45.5 %gather_fusion.3 = f32[8192]{0:T(1024)S(1)} fusion(f32[16384]{0:T(1024)S(1)} %bitcast.128, s32[8192]{0:T(1024)S(1)} %broadcast_clamp_fusion.1), kind=kCustom, calls=%fused_computation.3 | custom fusion | bytes 98304 | tf_op jit(solution)/shard_map/gather | solution.py:96
  552.9 10.8 %all-to-all-start.2 = ((f32[128,1,64]{2,1,0:T(1,128)}), f32[128,1,64]{2,1,0:T(1,128)S(1)}, u32[]{:S(2)}, u32[]{:S(2)}) async-start(f32[128,1,64]{2,1,0:T(1,128)} %bitcast.9), calls=%async_computation.2 | async-start | bytes 131072 | tf_op jit(solution)/shard_map/all_to_all | solution.py:99
  563.7 9.7 all-to-all-done.2
  578.5 44.9 %scatter_custom_fusion.3 = f32[8192]{0:T(1024)S(1)} fusion(s32[8192]{0:T(1024)S(1)} %reshape.483, f32[8192]{0:T(1024)S(1)} %reshape.605, f32[]{:T(128)} %constant.152.clone.1), kind=kCustom, calls=%fused_computation.360 | custom fusion | flops 8192 | bytes 32772 | tf_op jit(solution)/shard_map/scatter-add | solution.py:103
  623.6 50.3 %scatter_fusion.1 = f32[16384]{0:T(1024)S(1)} fusion(f32[16384]{0:T(1024)S(1)} %bitcast.129, s32[8192]{0:T(1024)S(1)} %reshape.579, f32[8192]{0:T(1024)S(1)} %reshape.597), kind=kCustom, calls=%fused_computation.15 | custom fusion | flops 8192 | bytes 131072 | tf_op jit(solution)/shard_map/scatter-add | solution.py:109
  681.6 9.8 collective-permute-start.36
  721.1 25.7 %all-gather.2 = f32[1,4096]{1,0:T(1,128)S(1)} all-gather(f32[1,256]{1,0:T(1,128)S(1)} %get-tuple-element.129), channel_id=4, replica_groups=mesh['row'=8,'col'=16] {'col'}, dimensions={1}, use_global_device_ids=true | all-gather | bytes 17408 | tf_op jit(solution)/shard_map/all_gather | solution.py:114
  760.9 45.5 %gather_fusion.10 = f32[8192]{0:T(1024)S(1)} fusion(f32[8192]{0:T(1024)S(1)} %bitcast.132, s32[8192]{0:T(1024)S(1)} %broadcast_clamp_fusion), kind=kCustom, calls=%fused_computation.10 | custom fusion | bytes 98304 | tf_op jit(solution)/shard_map/gather | solution.py:98
  819.3 45.5 %gather_fusion.7 = f32[8192]{0:T(1024)S(1)} fusion(f32[16384]{0:T(1024)S(1)} %bitcast.130, s32[8192]{0:T(1024)S(1)} %broadcast_clamp_fusion.1), kind=kCustom, calls=%fused_computation.7 | custom fusion | bytes 98304 | tf_op jit(solution)/shard_map/gather | solution.py:96
  865.5 10.8 %all-to-all-start.5 = ((f32[128,1,64]{2,1,0:T(1,128)}), f32[128,1,64]{2,1,0:T(1,128)S(1)}, u32[]{:S(2)}, u32[]{:S(2)}) async-start(f32[128,1,64]{2,1,0:T(1,128)} %bitcast.28), calls=%async_computation.5 | async-start | bytes 131072 | tf_op jit(solution)/shard_map/all_to_all | solution.py:99
  876.4 9.7 all-to-all-done.5
  886.2 44.9 %scatter_custom_fusion.5 = f32[8192]{0:T(1024)S(1)} fusion(s32[8192]{0:T(1024)S(1)} %reshape.483, f32[8192]{0:T(1024)S(1)} %reshape.621, f32[]{:T(128)} %constant.152.clone.1), kind=kCustom, calls=%fused_computation.358 | custom fusion | flops 8192 | bytes 32772 | tf_op jit(solution)/shard_map/scatter-add | solution.py:103
  932.4 9.8 all-to-all-start.7
  943.0 8.9 all-to-all-done.7
  952.0 50.3 %scatter_fusion.2 = f32[16384]{0:T(1024)S(1)} fusion(f32[16384]{0:T(1024)S(1)} %bitcast.131, s32[8192]{0:T(1024)S(1)} %reshape.579, f32[8192]{0:T(1024)S(1)} %reshape.613), kind=kCustom, calls=%fused_computation.17 | custom fusion | flops 8192 | bytes 131072 | tf_op jit(solution)/shard_map/scatter-add | solution.py:109
  (289 shorter events, 242.7 us)
Async XLA Ops:
  1.4 24.6 %collective-permute-start.2 = (f32[1,256]{1,0:T(1,128)S(1)}, f32[1,256]{1,0:T(1,128)S(1)}, u32[]{:S(2)}, u32[]{:S(2)}) collective-permute-start(f32[1,256]{1,0:T(1,128)S(1)} %get-tuple-element.127), channel_id=1, source_target_pairs={{16,0},{32,16},{48,32},{64,48},{80,64},{96,80},{112,96},{17,1},{33... | collective-permute-start | bytes 3080 | tf_op jit(solution)/shard_map/ppermute | solution.py:31
  4.7 21.3 %collective-permute-start.1 = (f32[1,256]{1,0:T(1,128)S(1)}, f32[1,256]{1,0:T(1,128)S(1)}, u32[]{:S(2)}, u32[]{:S(2)}) collective-permute-start(f32[1,256]{1,0:T(1,128)S(1)} %get-tuple-element.126), channel_id=1, source_target_pairs={{0,16},{16,32},{32,48},{48,64},{64,80},{80,96},{96,112},{1,17},{17... | collective-permute-start | bytes 3080 | tf_op jit(solution)/shard_map/ppermute | solution.py:28
  8.5 23.2 %collective-permute-start = (f32[1,256]{1,0:T(1,128)S(1)}, f32[1,256]{1,0:T(1,128)S(1)}, u32[]{:S(2)}, u32[]{:S(2)}) collective-permute-start(f32[1,256]{1,0:T(1,128)S(1)} %slice.500), channel_id=1, source_target_pairs={{0,16},{16,32},{32,48},{48,64},{64,80},{80,96},{96,112},{1,17},{17... | collective-permute-start | bytes 3080 | tf_op jit(solution)/shard_map/ppermute | solution.py:20
  11.9 19.8 %collective-permute-start.3 = (f32[64,1]{1,0:T(8,128)S(1)}, f32[64,1]{1,0:T(8,128)S(1)}, u32[]{:S(2)}, u32[]{:S(2)}) collective-permute-start(f32[64,1]{1,0:T(8,128)S(1)} %slice.506), channel_id=1, source_target_pairs={{0,1},{1,2},{2,3},{3,4},{4,5},{5,6},{6,7},{7,8},{8,9},{9,10},{10,1... | collective-permute-start | bytes 776 | tf_op jit(solution)/shard_map/ppermute | solution.py:20
  15.8 226.5 %all-to-all-start.3 = ((f32[16,256,1]{1,2,0:T(1,128)}), f32[16,256,1]{1,2,0:T(1,128)S(1)}, u32[]{:S(2)}, u32[]{:S(2)}) async-start(f32[16,256,1]{1,2,0:T(1,128)} %concatenate.271), calls=%async_computation.3 | async-start | bytes 32768 | tf_op jit(solution)/shard_map/all_to_all | solution.py:14
  40.3 30.4 %collective-permute-start.9 = (f32[66,1]{1,0:T(8,128)S(1)}, f32[66,1]{1,0:T(8,128)S(1)}, u32[]{:S(2)}, u32[]{:S(2)}) collective-permute-start(f32[66,1]{1,0:T(8,128)S(1)} %get-tuple-element.101), channel_id=1, source_target_pairs={{1,0},{2,1},{3,2},{4,3},{5,4},{6,5},{7,6},{8,7},{9,8},{10,9},{11,1... | collective-permute-start | bytes 800 | tf_op jit(solution)/shard_map/ppermute | solution.py:31
  41.6 29.1 %collective-permute-start.8 = (f32[66,1]{1,0:T(8,128)S(1)}, f32[66,1]{1,0:T(8,128)S(1)}, u32[]{:S(2)}, u32[]{:S(2)}) collective-permute-start(f32[66,1]{1,0:T(8,128)S(1)} %get-tuple-element.100), channel_id=1, source_target_pairs={{0,1},{1,2},{2,3},{3,4},{4,5},{5,6},{6,7},{7,8},{8,9},{9,10},{10,1... | collective-permute-start | bytes 800 | tf_op jit(solution)/shard_map/ppermute | solution.py:28
  90.3 54.0 %collective-permute-start.15 = (f32[1,256]{1,0:T(1,128)S(1)}, f32[1,256]{1,0:T(1,128)S(1)}, u32[]{:S(2)}, u32[]{:S(2)}) collective-permute-start(f32[1,256]{1,0:T(1,128)S(1)} %get-tuple-element.121), channel_id=1, source_target_pairs={{16,0},{32,16},{48,32},{64,48},{80,64},{96,80},{112,96},{17,1},{33... | collective-permute-start | bytes 3080 | tf_op jit(solution)/shard_map/ppermute | solution.py:31
  92.2 52.0 %collective-permute-start.14 = (f32[1,256]{1,0:T(1,128)S(1)}, f32[1,256]{1,0:T(1,128)S(1)}, u32[]{:S(2)}, u32[]{:S(2)}) collective-permute-start(f32[1,256]{1,0:T(1,128)S(1)} %get-tuple-element.120), channel_id=1, source_target_pairs={{0,16},{16,32},{32,48},{48,64},{64,80},{80,96},{96,112},{1,17},{17... | collective-permute-start | bytes 3080 | tf_op jit(solution)/shard_map/ppermute | solution.py:28
  144.4 51.5 %collective-permute-start.17 = (f32[66,1]{1,0:T(8,128)S(1)}, f32[66,1]{1,0:T(8,128)S(1)}, u32[]{:S(2)}, u32[]{:S(2)}) collective-permute-start(f32[66,1]{1,0:T(8,128)S(1)} %get-tuple-element.97), channel_id=1, source_target_pairs={{1,0},{2,1},{3,2},{4,3},{5,4},{6,5},{7,6},{8,7},{9,8},{10,9},{11,1... | collective-permute-start | bytes 800 | tf_op jit(solution)/shard_map/ppermute | solution.py:31
  145.7 50.3 %collective-permute-start.16 = (f32[66,1]{1,0:T(8,128)S(1)}, f32[66,1]{1,0:T(8,128)S(1)}, u32[]{:S(2)}, u32[]{:S(2)}) collective-permute-start(f32[66,1]{1,0:T(8,128)S(1)} %get-tuple-element.96), channel_id=1, source_target_pairs={{0,1},{1,2},{2,3},{3,4},{4,5},{5,6},{6,7},{7,8},{8,9},{9,10},{10,1... | collective-permute-start | bytes 800 | tf_op jit(solution)/shard_map/ppermute | solution.py:28
  261.4 49.4 %all-to-all-start.1 = ((f32[128,1,64]{2,1,0:T(1,128)}), f32[128,1,64]{2,1,0:T(1,128)S(1)}, u32[]{:S(2)}, u32[]{:S(2)}) async-start(f32[128,1,64]{2,1,0:T(1,128)} %bitcast.5), calls=%async_computation.1 | async-start | bytes 131072 | tf_op jit(solution)/shard_map/all_to_all | solution.py:104
  402.6 33.3 %collective-permute-start.29 = (f32[66,1]{1,0:T(8,128)S(1)}, f32[66,1]{1,0:T(8,128)S(1)}, u32[]{:S(2)}, u32[]{:S(2)}) collective-permute-start(f32[66,1]{1,0:T(8,128)S(1)} %get-tuple-element.91), channel_id=1, source_target_pairs={{1,0},{2,1},{3,2},{4,3},{5,4},{6,5},{7,6},{8,7},{9,8},{10,9},{11,1... | collective-permute-start | bytes 800 | tf_op jit(solution)/shard_map/ppermute | solution.py:31
  403.8 32.0 %collective-permute-start.28 = (f32[66,1]{1,0:T(8,128)S(1)}, f32[66,1]{1,0:T(8,128)S(1)}, u32[]{:S(2)}, u32[]{:S(2)}) collective-permute-start(f32[66,1]{1,0:T(8,128)S(1)} %get-tuple-element.90), channel_id=1, source_target_pairs={{0,1},{1,2},{2,3},{3,4},{4,5},{5,6},{6,7},{7,8},{8,9},{9,10},{10,1... | collective-permute-start | bytes 800 | tf_op jit(solution)/shard_map/ppermute | solution.py:28
  436.0 62.2 %collective-permute-start.31 = (f32[1,256]{1,0:T(1,128)S(1)}, f32[1,256]{1,0:T(1,128)S(1)}, u32[]{:S(2)}, u32[]{:S(2)}) collective-permute-start(f32[1,256]{1,0:T(1,128)S(1)} %get-tuple-element.113), channel_id=1, source_target_pairs={{16,0},{32,16},{48,32},{64,48},{80,64},{96,80},{112,96},{17,1},{33... | collective-permute-start | bytes 3080 | tf_op jit(solution)/shard_map/ppermute | solution.py:31
  441.2 57.1 %collective-permute-start.30 = (f32[1,256]{1,0:T(1,128)S(1)}, f32[1,256]{1,0:T(1,128)S(1)}, u32[]{:S(2)}, u32[]{:S(2)}) collective-permute-start(f32[1,256]{1,0:T(1,128)S(1)} %get-tuple-element.112), channel_id=1, source_target_pairs={{0,16},{16,32},{32,48},{48,64},{64,80},{80,96},{96,112},{1,17},{17... | collective-permute-start | bytes 3080 | tf_op jit(solution)/shard_map/ppermute | solution.py:28
  552.9 20.6 %all-to-all-start.2 = ((f32[128,1,64]{2,1,0:T(1,128)}), f32[128,1,64]{2,1,0:T(1,128)S(1)}, u32[]{:S(2)}, u32[]{:S(2)}) async-start(f32[128,1,64]{2,1,0:T(1,128)} %bitcast.9), calls=%async_computation.2 | async-start | bytes 131072 | tf_op jit(solution)/shard_map/all_to_all | solution.py:99
  574.1 49.4 %all-to-all-start.4 = ((f32[128,1,64]{2,1,0:T(1,128)}), f32[128,1,64]{2,1,0:T(1,128)S(1)}, u32[]{:S(2)}, u32[]{:S(2)}) async-start(f32[128,1,64]{2,1,0:T(1,128)} %bitcast.24), calls=%async_computation.4 | async-start | bytes 131072 | tf_op jit(solution)/shard_map/all_to_all | solution.py:104
  715.2 33.3 %collective-permute-start.45 = (f32[66,1]{1,0:T(8,128)S(1)}, f32[66,1]{1,0:T(8,128)S(1)}, u32[]{:S(2)}, u32[]{:S(2)}) collective-permute-start(f32[66,1]{1,0:T(8,128)S(1)} %get-tuple-element.83), channel_id=1, source_target_pairs={{1,0},{2,1},{3,2},{4,3},{5,4},{6,5},{7,6},{8,7},{9,8},{10,9},{11,1... | collective-permute-start | bytes 800 | tf_op jit(solution)/shard_map/ppermute | solution.py:31
  716.5 32.0 %collective-permute-start.44 = (f32[66,1]{1,0:T(8,128)S(1)}, f32[66,1]{1,0:T(8,128)S(1)}, u32[]{:S(2)}, u32[]{:S(2)}) collective-permute-start(f32[66,1]{1,0:T(8,128)S(1)} %get-tuple-element.82), channel_id=1, source_target_pairs={{0,1},{1,2},{2,3},{3,4},{4,5},{5,6},{6,7},{7,8},{8,9},{9,10},{10,1... | collective-permute-start | bytes 800 | tf_op jit(solution)/shard_map/ppermute | solution.py:28
  748.7 62.2 %collective-permute-start.47 = (f32[1,256]{1,0:T(1,128)S(1)}, f32[1,256]{1,0:T(1,128)S(1)}, u32[]{:S(2)}, u32[]{:S(2)}) collective-permute-start(f32[1,256]{1,0:T(1,128)S(1)} %get-tuple-element.105), channel_id=1, source_target_pairs={{16,0},{32,16},{48,32},{64,48},{80,64},{96,80},{112,96},{17,1},{33... | collective-permute-start | bytes 3080 | tf_op jit(solution)/shard_map/ppermute | solution.py:31
  753.9 57.1 %collective-permute-start.46 = (f32[1,256]{1,0:T(1,128)S(1)}, f32[1,256]{1,0:T(1,128)S(1)}, u32[]{:S(2)}, u32[]{:S(2)}) collective-permute-start(f32[1,256]{1,0:T(1,128)S(1)} %get-tuple-element.104), channel_id=1, source_target_pairs={{0,16},{16,32},{32,48},{48,64},{64,80},{80,96},{96,112},{1,17},{17... | collective-permute-start | bytes 3080 | tf_op jit(solution)/shard_map/ppermute | solution.py:28
  865.5 20.6 %all-to-all-start.5 = ((f32[128,1,64]{2,1,0:T(1,128)}), f32[128,1,64]{2,1,0:T(1,128)S(1)}, u32[]{:S(2)}, u32[]{:S(2)}) async-start(f32[128,1,64]{2,1,0:T(1,128)} %bitcast.28), calls=%async_computation.5 | async-start | bytes 131072 | tf_op jit(solution)/shard_map/all_to_all | solution.py:99
  932.4 19.5 %all-to-all-start.7 = ((f32[128,1,64]{2,1,0:T(1,128)}), f32[128,1,64]{2,1,0:T(1,128)S(1)}, u32[]{:S(2)}, u32[]{:S(2)}) async-start(f32[128,1,64]{2,1,0:T(1,128)} %bitcast.37), calls=%async_computation.7 | async-start | bytes 131072 | tf_op jit(solution)/shard_map/all_to_all | solution.py:104
  (48 other events, 362.5 us)
